TPU v7x, 32 devices: a whole 2x2x4 slice. The times are simulated.
32 devices in a mesh: plane: 4 (over y, x), tile: 8 (over z, core).
Axes of the slice: x: 2, y: 2, z: 4, core: 2. Of those that a mesh axis runs over, the one named last changes fastest.
Arguments:
- recording: bfloat16 [4, 8, 3, 4, 256, 128], P('plane', 'tile'), may hold values from -8 to 8
- start_vectors: float32 [4, 16, 32, 128], P('plane', 'tile'), may hold values from -5 to 5
- footprints: bfloat16 [4, 1024, 256], P('plane', 'tile'), may hold values from 0.00019931793 to 0.029907227
- source_row: int32 [4, 1024, 1], P('plane', 'tile'), may hold values from 0 to 5; in each aligned block of 128 rows (0 to 127, 128 to 255, ..., all dimensions but the last counted through in order) at most 32 rows name the same one
- footprint_block: int32 [4, 1024], P('plane', 'tile'), may hold values from 0 to 3
Outputs:
- temporal_factors: float32 [4, 16, 32, 128], P('plane', 'tile')
- traces: float32 [4, 1024, 128], P('plane', 'tile')
Inputs may be any that keep to these rules, and one draw needn't show every extreme that they name: `source_row`: among the 128 sources of one device at most 32 share a value, and some value is shared by exactly 32 of them.
All inputs are finite; a program needn't handle non-finite values.
Results may differ from a plain program's by a relative error of at most 0.0069.
Values may be sent and summed in bfloat16 or wider, within the bound.
No kernel may reach another device: no remote copies, remote signals or barrier semaphores. Data moves between devices by JAX's collectives and lax.ppermute only.
A program may use at most 64 MiB of HBM per device.

v0:
```python
import jax
import jax.numpy as jnp
from jax import lax
from jax.sharding import PartitionSpec as P

ITERS = 3


def from_behind(block, axis, distance):
    devices = range(lax.axis_size(axis))
    route = [(i - distance, i) for i in devices if i - distance in devices]
    return lax.ppermute(block, axis, route)


def compress_patches(patches, start_block):
    temporal = start_block
    spatial = None
    for step_index in range(ITERS):
        projection = jnp.einsum(
            "prf,pkf->prk",
            temporal.astype(jnp.bfloat16),
            patches,
            preferred_element_type=jnp.float32,
        )
        gram_matrix = jnp.einsum(
            "prk,psk->prs", projection, projection, precision=lax.Precision.HIGHEST
        )
        cholesky_factor = jnp.linalg.cholesky(gram_matrix)
        spatial = jax.scipy.linalg.solve_triangular(cholesky_factor, projection, lower=True).astype(
            jnp.bfloat16
        )
        temporal = jnp.einsum("prk,pkf->prf", spatial, patches, preferred_element_type=jnp.float32)
    return (spatial, temporal)


def on_device(recording, start_vectors, footprints, source_row, footprint_block):
    tile_count = lax.axis_size("tile")
    own_strip = recording[0, 0]
    cell_count = own_strip.shape[0]
    patch_count = cell_count - 1
    block_pixels = own_strip.shape[2]
    frame_count = own_strip.shape[3]
    pixel_total = lax.axis_size("plane") * tile_count * cell_count * 4 * block_pixels
    frame_sum = jnp.sum(own_strip, axis=(0, 1, 2), dtype=jnp.float32)
    background = lax.psum(frame_sum, ("plane", "tile")) / pixel_total
    centered = (own_strip.astype(jnp.float32) - background).astype(jnp.bfloat16)
    lower_strip = from_behind(centered, "tile", -2)
    stacked = jnp.stack([centered, lower_strip])
    patches = jnp.stack(
        [
            stacked[:, column_index : column_index + 2].reshape(16 * block_pixels, frame_count)
            for column_index in range(patch_count)
        ]
    )
    spatial, temporal = compress_patches(patches, start_vectors[0])
    rank_width = spatial.shape[1]
    temporal_rounded = temporal.astype(jnp.bfloat16)
    source_rows = source_row[0, :, 0]
    block_value = footprint_block[0]
    footprint_rows = footprints[0]
    source_count = source_rows.shape[0]
    row_span = tile_count - 2
    capacity = max(2, (3 * source_count + 2 * row_span - 1) // (2 * row_span))
    row_match = (source_rows[:, None] == jnp.arange(tile_count)[None, :]).astype(jnp.int32)
    position = jnp.sum(jnp.cumsum(row_match, axis=0) * row_match, axis=1) - 1
    slot_upper = source_rows * capacity + position
    slot_lower = (source_rows + 2) * capacity + position
    footprint_send = jnp.zeros((tile_count * capacity, 2, block_pixels), jnp.bfloat16)
    footprint_send = (
        footprint_send.at[slot_upper, 0].set(footprint_rows).at[slot_lower, 1].set(footprint_rows)
    )
    block_send = jnp.full((tile_count * capacity, 2), -1, jnp.int32)
    block_send = block_send.at[slot_upper, 0].set(block_value).at[slot_lower, 1].set(block_value)
    footprint_send = footprint_send.reshape(tile_count, capacity, 2, block_pixels)
    block_send = block_send.reshape(tile_count, capacity, 2)
    spatial_blocks = spatial.reshape(patch_count, rank_width, 16, block_pixels)
    patch_axis = jnp.arange(patch_count)[None, None, :, None]
    block_axis = jnp.arange(8)[None, None, None, :]
    footprint_in = lax.all_to_all(footprint_send, "tile", split_axis=0, concat_axis=0, tiled=True)
    codes_in = lax.all_to_all(block_send, "tile", split_axis=0, concat_axis=0, tiled=True)
    role_terms = []
    for half_index in range(2):
        strip_offset = 1 - half_index
        block_range = spatial_blocks[:, :, strip_offset * 8 : strip_offset * 8 + 8]
        projected = jnp.einsum(
            "nkb,prgb->nkpgr",
            footprint_in[:, :, half_index],
            block_range,
            preferred_element_type=jnp.float32,
        )
        block_codes = codes_in[:, :, half_index]
        column_cell = (block_codes // 4 + 1)[:, :, None, None]
        quarter = (block_codes % 4)[:, :, None, None]
        filled = (block_codes >= 0)[:, :, None, None]
        from_left = (patch_axis == column_cell - 1) & (block_axis == quarter + 4)
        from_right = (patch_axis == column_cell) & (block_axis == quarter)
        selector = ((from_left | from_right) & filled).astype(jnp.float32)
        coefficient = jnp.sum(selector[..., None] * projected, axis=3)
        role_terms.append(
            coefficient.reshape(
                coefficient.shape[0], coefficient.shape[1], patch_count * rank_width
            )
        )
    coefficient = jnp.stack(role_terms, 2).astype(jnp.bfloat16)
    replies = lax.all_to_all(coefficient, "tile", split_axis=0, concat_axis=0, tiled=True)
    reply_rows = replies.reshape(tile_count * capacity, 2, patch_count * rank_width)
    upper_coefs = reply_rows[slot_upper, 0].reshape(source_count, patch_count, rank_width)
    lower_coefs = reply_rows[slot_lower, 1].reshape(source_count, patch_count, rank_width)
    coef_table = jnp.concatenate(
        [upper_coefs, lower_coefs, jnp.zeros((source_count, 1, rank_width), jnp.bfloat16)], 1
    )
    shard_rows = lax.all_gather(temporal_rounded, "tile", axis=0, tiled=True)
    patch_number = shard_rows.shape[0]
    patch_index = jnp.arange(patch_number)
    owner_row = patch_index // patch_count
    patch_column = patch_index % patch_count
    lookup = jnp.where(
        owner_row[None, :] == source_rows[:, None],
        patch_column[None, :],
        jnp.where(
            owner_row[None, :] == source_rows[:, None] + 2,
            patch_count + patch_column[None, :],
            2 * patch_count,
        ),
    )
    weights = jnp.take_along_axis(coef_table, lookup[:, :, None], axis=1)
    weights = weights.reshape(source_count, patch_number * rank_width)
    summed = jnp.dot(
        weights,
        shard_rows.reshape(patch_number * rank_width, frame_count),
        preferred_element_type=jnp.float32,
    )
    traces = 0.25 * summed
    return (temporal[None], traces[None])


def solution(mesh):
    placed = (
        P("plane", "tile", None, None, None, None),
        P("plane", "tile", None, None),
        P("plane", "tile", None),
        P("plane", "tile", None),
        P("plane", "tile"),
    )
    return jax.shard_map(
        on_device,
        mesh=mesh,
        in_specs=placed,
        out_specs=(P("plane", "tile", None, None), P("plane", "tile", None)),
        check_vma=False,
    )
```

profile of v0, /device:TPU:0, one launch (start us, length us, event | category | flops | bytes accessed | tf_op | source)
XLA Modules:
  0.0 174.9 jit_solution(6968167123436777132)
XLA Ops:
  0.6 1.6 convert_reduce_fusion
  2.3 42.0 %psum.7 = f32[128]{0:T(128)S(1)} all-reduce(f32[128]{0:T(128)S(1)} %convert_reduce_fusion), channel_id=1, replica_groups=mesh['plane'=4,'tile'=8] {'plane','tile'}, use_global_device_ids=true, to_apply=%region_1.0 | all-reduce | flops 128 | bytes 1024 | tf_op jit(solution)/shard_map/psum | solution.py:45
  44.3 0.2 fusion.5
  44.5 1.3 collective-permute-start
  45.8 0.1 fusion.18
  45.9 0.2 reduce_window_sum.11
  46.1 0.2 select_reduce_fusion
  46.3 6.8 %scatter_fusion = s32[256,2]{0,1:T(2,128)S(1)} fusion(s32[256,2]{0,1:T(2,128)S(1)} %broadcast_in_dim.81, s32[128]{0:T(128)S(1)} %get-tuple-element.28, s32[128]{0:T(128)S(1)} %bitcast.186), kind=kCustom, calls=%fused_computation.3 | custom fusion | bytes 2560 | tf_op jit(solution)/shard_map/scatter | solution.py:73
  53.2 6.8 %scatter_fusion.1 = s32[256,2]{0,1:T(2,128)S(1)} fusion(s32[256,2]{0,1:T(2,128)S(1)} %scatter_fusion, s32[128]{0:T(128)S(1)} %get-tuple-element.29, s32[128]{0:T(128)S(1)} %bitcast.187), kind=kCustom, calls=%fused_computation.4 | custom fusion | bytes 2560 | tf_op jit(solution)/shard_map/scatter | solution.py:73
  60.1 0.6 copy.50
  60.7 5.7 %all-to-all-start = ((s32[8,32,2]{1,2,0:T(2,128)}), s32[8,32,2]{1,2,0:T(2,128)S(1)}, u32[]{:S(2)}, u32[]{:S(2)}) async-start(s32[8,32,2]{1,2,0:T(2,128)} %copy.50), calls=%async_computation | async-start | bytes 16384 | tf_op jit(solution)/shard_map/all_to_all | solution.py:80
  66.5 0.2 fusion.3
  66.7 0.1 fusion.16
  66.8 0.1 compare_and_fusion
  66.9 0.1 broadcast_in_dim.82
  67.1 6.8 %scatter_fusion.2 = bf16[256,2,256]{2,1,0:T(2,128)(2,1)S(1)} fusion(bf16[256,2,256]{2,1,0:T(2,128)(2,1)S(1)} %broadcast_in_dim.82, s32[128]{0:T(128)S(1)} %get-tuple-element.28, bf16[128,256]{1,0:T(8,128)(2,1)S(1)} %bitcast.172), kind=kCustom, calls=%fused_computation.5 | custom fusion | bytes 197632 | tf_op jit(solution)/shard_map/scatter | solution.py:70
  73.9 6.8 %scatter_fusion.3 = bf16[256,2,256]{2,1,0:T(2,128)(2,1)S(1)} fusion(bf16[256,2,256]{2,1,0:T(2,128)(2,1)S(1)} %scatter_fusion.2, s32[128]{0:T(128)S(1)} %get-tuple-element.29, bf16[128,256]{1,0:T(8,128)(2,1)S(1)} %bitcast.173), kind=kCustom, calls=%fused_computation.6 | custom fusion | bytes 197632 | tf_op jit(solution)/shard_map/scatter | solution.py:70
  80.7 0.8 copy.52
  81.5 0.1 reshape.577
  81.6 5.1 %all-to-all-start.1 = ((bf16[8,32,2,256]{3,1,2,0:T(8,128)(2,1)}), bf16[8,32,2,256]{3,1,2,0:T(8,128)(2,1)}, u32[]{:S(2)}, u32[]{:S(2)}) async-start(bf16[8,32,2,256]{3,1,2,0:T(8,128)(2,1)} %copy.52), calls=%async_computation.1 | async-start | bytes 524288 | tf_op jit(solution)/shard_map/all_to_all | solution.py:79
  87.0 0.7 and_convert_fusion.1
  87.6 0.2 fusion.10
  87.8 0.6 copy-done.7
  88.4 0.8 fusion.25
  89.2 1.1 fusion.41
  90.4 5.9 %custom-call.24 = f32[2,32,32]{2,1,0:T(8,128)S(1)} custom-call(f32[2,32,32]{2,1,0:T(8,128)S(1)} %fusion.24), custom_call_target="Cholesky" | custom-call | tf_op jit(solution)/shard_map/jit(cholesky)/cholesky | solution.py:28
  96.3 0.1 compare_reduce_fusion.2
  96.4 0.1 select_bitcast_fusion.2
  96.5 4.9 %custom-call.25 = f32[2,1,32,32]{2,3,1,0:T(8,128)S(1)} custom-call(f32[2,1,32,32]{3,2,1,0:T(8,128)S(1)} %select_bitcast_fusion.2), custom_call_target="InvertDiagBlocksLowerTriangular" | custom-call | tf_op jit(solution)/shard_map/jit(_solve_triangular)/vmap()/triangular_solve | solution.py:29
  101.4 1.1 convolution_convert_fusion.2
  102.5 2.7 %fusion.8 = f32[2,32,4096]{2,1,0:T(8,128)S(1)} fusion(bf16[2,32,4096]{2,1,0:T(8,128)(2,1)S(1)} %convolution_convert_fusion.2, bf16[1,4096,128]{2,1,0:T(8,128)(2,1)} %bitcast.165, bf16[1,4096,128]{2,1,0:T(8,128)(2,1)S(1)} %bitcast.161), kind=kOutput, calls=%fused_computation.29 | convolution fusion | flops 136323072 | bytes 3670016 | tf_op jit(solution)/shard_map/prf,pkf->prk/dot_general | solution.py:19
  105.2 1.1 fusion.42
  106.4 5.9 %custom-call.26 = f32[2,32,32]{2,1,0:T(8,128)S(1)} custom-call(f32[2,32,32]{2,1,0:T(8,128)S(1)} %fusion.22), custom_call_target="Cholesky" | custom-call | tf_op jit(solution)/shard_map/jit(cholesky)/cholesky | solution.py:28
  112.3 0.1 compare_reduce_fusion.1
  112.4 0.1 select_bitcast_fusion.1
  112.5 4.9 %custom-call.27 = f32[2,1,32,32]{2,3,1,0:T(8,128)S(1)} custom-call(f32[2,1,32,32]{3,2,1,0:T(8,128)S(1)} %select_bitcast_fusion.1), custom_call_target="InvertDiagBlocksLowerTriangular" | custom-call | tf_op jit(solution)/shard_map/jit(_solve_triangular)/vmap()/triangular_solve | solution.py:29
  117.4 1.1 convolution_convert_fusion.1
  118.5 2.7 %fusion.9 = f32[2,32,4096]{2,1,0:T(8,128)S(1)} fusion(bf16[2,32,4096]{2,1,0:T(8,128)(2,1)S(1)} %convolution_convert_fusion.1, bf16[1,4096,128]{2,1,0:T(8,128)(2,1)} %bitcast.166, bf16[1,4096,128]{2,1,0:T(8,128)(2,1)S(1)} %bitcast.162), kind=kOutput, calls=%fused_computation.30 | convolution fusion | flops 136323072 | bytes 3670016 | tf_op jit(solution)/shard_map/prf,pkf->prk/dot_general | solution.py:19
  121.2 1.1 fusion.43
  122.4 5.9 %custom-call.28 = f32[2,32,32]{2,1,0:T(8,128)S(1)} custom-call(f32[2,32,32]{2,1,0:T(8,128)S(1)} %fusion.20), custom_call_target="Cholesky" | custom-call | tf_op jit(solution)/shard_map/jit(cholesky)/cholesky | solution.py:28
  128.3 0.1 compare_reduce_fusion
  128.4 0.1 select_bitcast_fusion
  128.5 5.1 %custom-call.29 = f32[2,1,32,32]{2,3,1,0:T(8,128)S(1)} custom-call(f32[2,1,32,32]{3,2,1,0:T(8,128)S(1)} %select_bitcast_fusion), custom_call_target="InvertDiagBlocksLowerTriangular" | custom-call | tf_op jit(solution)/shard_map/jit(_solve_triangular)/vmap()/triangular_solve | solution.py:29
  133.6 1.0 convolution_convert_fusion
  134.6 0.1 copy.75
  134.8 1.7 fusion
  136.5 0.1 copy.71
  136.7 1.8 %fusion.1 = bf16[8,32,2,32]{1,0,3,2:T(8,128)(2,1)S(1)} fusion(f32[8,32,2,8]{1,3,0,2:T(8,128)S(1)} %copy-done.4, bf16[2,32,16,256]{3,2,1,0:T(8,128)(2,1)S(1)} %bitcast.170, bf16[8,32,2,256]{3,1,2,0:T(8,128)(2,1)} %all-to-all-done.1), kind=kOutput, calls=%fused_computation.17 | convolution fusion | flops 67354624 | bytes 491520 | tf_op jit(solution)/shard_map/nkb,prgb->nkpgr/dot_general | solution.py:85
  138.5 0.1 copy.70
  138.7 0.8 reshape.613
  139.5 5.1 %all-to-all-start.2 = ((bf16[8,2,2048]{2,1,0:T(2,128)(2,1)}), bf16[8,2,2048]{2,1,0:T(2,128)(2,1)S(1)}, u32[]{:S(2)}, u32[]{:S(2)}) async-start(bf16[8,2,2048]{2,1,0:T(2,128)(2,1)} %reshape.613), calls=%async_computation.2 | async-start | bytes 131072 | tf_op jit(solution)/shard_map/all_to_all | solution.py:105
  144.6 1.1 fusion.40
  145.7 14.5 %all_gather.3 = bf16[16,32,128]{2,1,0:T(8,128)(2,1)S(1)} all-gather(bf16[2,32,128]{2,1,0:T(8,128)(2,1)S(1)} %get-tuple-element.26), channel_id=1, replica_groups=mesh['plane'=4,'tile'=8] {'tile'}, dimensions={0}, use_global_device_ids=true | all-gather | bytes 147456 | tf_op jit(solution)/shard_map/all_gather | solution.py:112
  160.2 0.1 reshape.614
  160.3 0.1 copy.58
  160.4 1.0 gather_fusion.1
  161.5 0.1 copy.60
  161.6 1.0 gather_fusion
  162.6 0.1 copy.59
  162.7 0.1 maximum_maximum_fusion
  162.8 0.2 copy.61
  163.0 10.6 %gather_fusion.2 = bf16[2048,32]{1,0:T(8,128)(2,1)S(1)} fusion(bf16[128,5,32]{2,0,1:T(8,128)(2,1)S(1)} %copy.61, s32[2048]{0:T(1024)S(1)} %reshape.577), kind=kCustom, calls=%fused_computation.2 | custom fusion | bytes 278528 | tf_op jit(solution)/shard_map/jit(take_along_axis)/gather | solution.py:126
  173.5 0.4 copy.62
  174.0 0.9 fusion.7
  (54 shorter events, 0.8 us)
Async XLA Ops:
  0.6 43.7 %copy-start = (bf16[1,1,3,4,256,128]{5,4,3,2,1,0:T(8,128)(2,1)S(1)}, bf16[1,1,3,4,256,128]{5,4,3,2,1,0:T(8,128)(2,1)}, u32[]{:S(2)}) copy-start(bf16[1,1,3,4,256,128]{5,4,3,2,1,0:T(8,128)(2,1)} %param.8) | copy-start | bytes 2359300
  0.6 45.2 %copy-start.5 = (s32[1,128,1]{1,2,0:T(1,128)S(1)}, s32[1,128,1]{1,2,0:T(1,128)}, u32[]{:S(2)}) copy-start(s32[1,128,1]{1,2,0:T(1,128)} %param.11) | copy-start | bytes 1540
  2.3 44.0 %copy-start.6 = (s32[1,128]{1,0:T(1,128)S(1)}, s32[1,128]{1,0:T(1,128)}, u32[]{:S(2)}) copy-start(s32[1,128]{1,0:T(1,128)} %param.12) | copy-start | bytes 1540
  44.5 43.1 %collective-permute-start = (bf16[3,4,256,128]{3,2,1,0:T(8,128)(2,1)S(1)}, bf16[3,4,256,128]{3,2,1,0:T(8,128)(2,1)S(1)}, u32[]{:S(2)}, u32[]{:S(2)}) collective-permute-start(bf16[3,4,256,128]{3,2,1,0:T(8,128)(2,1)S(1)} %fusion.5), channel_id=1, source_target_pairs={{2,0},{3,1},{4,2},{5,3},{6,4},{7,5},{10,8},{11,9},{12,10},{13,11},... | collective-permute-start | bytes 2359304 | tf_op jit(solution)/shard_map/ppermute | solution.py:12
  60.0 7.0 %copy-start.3 = (bf16[1,128,256]{2,1,0:T(8,128)(2,1)S(1)}, bf16[1,128,256]{2,1,0:T(8,128)(2,1)}, u32[]{:S(2)}) copy-start(bf16[1,128,256]{2,1,0:T(8,128)(2,1)} %param.10) | copy-start | bytes 196612
  60.7 20.9 %all-to-all-start = ((s32[8,32,2]{1,2,0:T(2,128)}), s32[8,32,2]{1,2,0:T(2,128)S(1)}, u32[]{:S(2)}, u32[]{:S(2)}) async-start(s32[8,32,2]{1,2,0:T(2,128)} %copy.50), calls=%async_computation | async-start | bytes 16384 | tf_op jit(solution)/shard_map/all_to_all | solution.py:80
  81.6 53.1 %all-to-all-start.1 = ((bf16[8,32,2,256]{3,1,2,0:T(8,128)(2,1)}), bf16[8,32,2,256]{3,1,2,0:T(8,128)(2,1)}, u32[]{:S(2)}, u32[]{:S(2)}) async-start(bf16[8,32,2,256]{3,1,2,0:T(8,128)(2,1)} %copy.52), calls=%async_computation.1 | async-start | bytes 524288 | tf_op jit(solution)/shard_map/all_to_all | solution.py:79
  87.6 0.8 copy-start.7
  87.8 1.4 copy-start.1
  134.8 1.9 %copy-start.4 = (f32[8,32,2,8]{1,3,0,2:T(8,128)S(1)}, f32[8,32,2,8]{1,3,0,2:T(8,128)}, u32[]{:S(2)}) copy-start(f32[8,32,2,8]{1,3,0,2:T(8,128)} %and_convert_fusion.1) | copy-start | bytes 49156
  136.7 7.9 %copy-start.2 = (bf16[2,2,4,256,128]{4,3,2,1,0:T(8,128)(2,1)S(1)}, bf16[2,2,4,256,128]{4,3,2,1,0:T(8,128)(2,1)}, u32[]{:S(2)}) copy-start(bf16[2,2,4,256,128]{4,3,2,1,0:T(8,128)(2,1)} %copy-done.1) | copy-start | bytes 3145732
  139.5 20.7 %all-to-all-start.2 = ((bf16[8,2,2048]{2,1,0:T(2,128)(2,1)}), bf16[8,2,2048]{2,1,0:T(2,128)(2,1)S(1)}, u32[]{:S(2)}, u32[]{:S(2)}) async-start(bf16[8,2,2048]{2,1,0:T(2,128)(2,1)} %reshape.613), calls=%async_computation.2 | async-start | bytes 131072 | tf_op jit(solution)/shard_map/all_to_all | solution.py:105
where the time goes:
time: 175 us
  blocking collectives  56.5 us (32%)
  local copies, waits for them, and re-layouts  44.8 us (26%)
  other arithmetic  37 us (21%)
  matrix products  18.2 us (10%)
  starting transfers between devices  17.2 us (10%)
    psum x1, blocking collectives, on_device(): background = lax.psum(frame_sum, ('plane', 'tile')) / pixel_total  42 us
    another operation x10, other arithmetic, compress_patches(): cholesky_factor = jnp.linalg.cholesky(gram_matrix)  18.1 us
    another operation x7, other arithmetic, compress_patches(): jax.scipy.linalg.solve_triangular(cholesky_factor, projection, lower=True)  15.2 us
    all_gather x1, blocking collectives, on_device(): shard_rows = lax.all_gather(temporal_rounded, 'tile', axis=0, tiled=True)  14.5 us
    scatter x2, local copies, waits for them, and re-layouts, on_device(): block_send.at[slot_upper, 0].set(block_value).at[slot_lower, 1]  13.7 us
    scatter x2, local copies, waits for them, and re-layouts, on_device(): footprint_send.at[slot_upper, 0].set(footprint_rows).at[slot_lower, 1]  13.6 us
    gather x3, local copies, waits for them, and re-layouts, on_device(): weights = jnp.take_along_axis(coef_table, lookup[:, :, None], axis=1)  11.1 us
    dot_general x3, matrix products, compress_patches(): jnp.einsum('prf,pkf->prk', temporal.astype(jnp.bfloat16), patches, prefer...  6.26 us
  transfers between devices with their start and end apart: 4, of which 0 were waited for; matrix products, arithmetic and copies ran while one was open for 45% of the time, Pallas kernels for 0%

commit v1 on v0

--- a/solution.py
+++ b/solution.py
@@ -4,6 +4,11 @@
 from jax.sharding import PartitionSpec as P
 
 ITERS = 3
+
+
+def summed_here(value, axis):
+    parts = lax.all_gather(value, axis)
+    return jnp.sum(parts, axis=0)
 
 
 def from_behind(block, axis, distance):
@@ -42,7 +47,7 @@
     frame_count = own_strip.shape[3]
     pixel_total = lax.axis_size("plane") * tile_count * cell_count * 4 * block_pixels
     frame_sum = jnp.sum(own_strip, axis=(0, 1, 2), dtype=jnp.float32)
-    background = lax.psum(frame_sum, ("plane", "tile")) / pixel_total
+    background = summed_here(frame_sum, ("plane", "tile")) / pixel_total
     centered = (own_strip.astype(jnp.float32) - background).astype(jnp.bfloat16)
     lower_strip = from_behind(centered, "tile", -2)
     stacked = jnp.stack([centered, lower_strip])

time: 175 us -> 175 us (level)
  starting transfers between devices: 17.2 us -> 15.4 us
    all_gather x0 -> x1, blocking collectives: none -> 43.1 us  [summed_here(): parts = lax.all_gather(value, axis)]
    psum x1 -> x0, blocking collectives: 42 us -> none  [on_device(): background = lax.psum(frame_sum, ('plane', 'tile')) / pixel_total]
    all_to_all x1, starting transfers between devices: 5.73 us -> 3.92 us  [on_device(): lax.all_to_all(block_send, 'tile', split_axis=0, concat_axis=0, tiled=True)]
where the time goes in v1:
time: 175 us; the launch traced here: 174 us
  blocking collectives  57.6 us (33%)
  local copies, waits for them, and re-layouts  44.8 us (26%)
  other arithmetic  37.1 us (21%)
  matrix products  18.2 us (10%)
  starting transfers between devices  15.4 us (9%)
    all_gather x1, blocking collectives, summed_here(): parts = lax.all_gather(value, axis)  43.1 us
    another operation x10, other arithmetic, compress_patches(): cholesky_factor = jnp.linalg.cholesky(gram_matrix)  18.1 us
    another operation x7, other arithmetic, compress_patches(): jax.scipy.linalg.solve_triangular(cholesky_factor, projection, lower=True)  15.2 us
    all_gather x1, blocking collectives, on_device(): shard_rows = lax.all_gather(temporal_rounded, 'tile', axis=0, tiled=True)  14.5 us
    scatter x2, local copies, waits for them, and re-layouts, on_device(): block_send.at[slot_upper, 0].set(block_value).at[slot_lower, 1]  13.7 us
    scatter x2, local copies, waits for them, and re-layouts, on_device(): footprint_send.at[slot_upper, 0].set(footprint_rows).at[slot_lower, 1]  13.6 us
    gather x3, local copies, waits for them, and re-layouts, on_device(): weights = jnp.take_along_axis(coef_table, lookup[:, :, None], axis=1)  11.1 us
    dot_general x3, matrix products, compress_patches(): jnp.einsum('prf,pkf->prk', temporal.astype(jnp.bfloat16), patches, prefer...  6.26 us
  transfers between devices with their start and end apart: 4, of which 0 were waited for; matrix products, arithmetic and copies ran while one was open for 45% of the time, Pallas kernels for 0%

profile of v1, /device:TPU:0, one launch (start us, length us, event | category | flops | bytes accessed | tf_op | source)
XLA Modules:
  0.0 174.1 jit_solution(17476929599759178963)
XLA Ops:
  0.6 1.6 convert_reduce_fusion
  2.3 43.1 %all-gather.1 = f32[32,1,128]{2,1,0:T(1,128)S(1)} all-gather(f32[1,1,128]{2,1,0:T(1,128)S(1)} %bitcast.189), channel_id=2, replica_groups=mesh['plane'=4,'tile'=8] {'plane','tile'}, dimensions={0}, use_global_device_ids=true | all-gather | bytes 16896 | tf_op jit(solution)/shard_map/all_gather | solution.py:10
  45.4 0.2 fusion.5
  45.6 1.3 collective-permute-start
  46.9 0.1 fusion.18
  47.0 0.2 reduce_window_sum.11
  47.2 0.2 select_reduce_fusion
  47.4 6.8 %scatter_fusion = s32[256,2]{0,1:T(2,128)S(1)} fusion(s32[256,2]{0,1:T(2,128)S(1)} %broadcast_in_dim.81, s32[128]{0:T(128)S(1)} %get-tuple-element.28, s32[128]{0:T(128)S(1)} %bitcast.187), kind=kCustom, calls=%fused_computation.3 | custom fusion | bytes 2560 | tf_op jit(solution)/shard_map/scatter | solution.py:78
  54.3 6.8 %scatter_fusion.1 = s32[256,2]{0,1:T(2,128)S(1)} fusion(s32[256,2]{0,1:T(2,128)S(1)} %scatter_fusion, s32[128]{0:T(128)S(1)} %get-tuple-element.29, s32[128]{0:T(128)S(1)} %bitcast.188), kind=kCustom, calls=%fused_computation.4 | custom fusion | bytes 2560 | tf_op jit(solution)/shard_map/scatter | solution.py:78
  61.1 0.1 reshape.560
  61.2 0.6 copy.50
  61.8 3.9 %all-to-all-start = ((s32[8,32,2]{1,2,0:T(2,128)}), s32[8,32,2]{1,2,0:T(2,128)S(1)}, u32[]{:S(2)}, u32[]{:S(2)}) async-start(s32[8,32,2]{1,2,0:T(2,128)} %copy.50), calls=%async_computation | async-start | bytes 16384 | tf_op jit(solution)/shard_map/all_to_all | solution.py:85
  65.7 0.2 fusion.3
  66.0 0.1 fusion.16
  66.1 0.1 compare_and_fusion
  66.2 0.1 broadcast_in_dim.82
  66.4 6.8 %scatter_fusion.2 = bf16[256,2,256]{2,1,0:T(2,128)(2,1)S(1)} fusion(bf16[256,2,256]{2,1,0:T(2,128)(2,1)S(1)} %broadcast_in_dim.82, s32[128]{0:T(128)S(1)} %get-tuple-element.28, bf16[128,256]{1,0:T(8,128)(2,1)S(1)} %bitcast.173), kind=kCustom, calls=%fused_computation.5 | custom fusion | bytes 197632 | tf_op jit(solution)/shard_map/scatter | solution.py:75
  73.2 6.8 %scatter_fusion.3 = bf16[256,2,256]{2,1,0:T(2,128)(2,1)S(1)} fusion(bf16[256,2,256]{2,1,0:T(2,128)(2,1)S(1)} %scatter_fusion.2, s32[128]{0:T(128)S(1)} %get-tuple-element.29, bf16[128,256]{1,0:T(8,128)(2,1)S(1)} %bitcast.174), kind=kCustom, calls=%fused_computation.6 | custom fusion | bytes 197632 | tf_op jit(solution)/shard_map/scatter | solution.py:75
  80.0 0.8 copy.52
  80.8 0.1 reshape.579
  80.9 5.1 %all-to-all-start.1 = ((bf16[8,32,2,256]{3,1,2,0:T(8,128)(2,1)}), bf16[8,32,2,256]{3,1,2,0:T(8,128)(2,1)}, u32[]{:S(2)}, u32[]{:S(2)}) async-start(bf16[8,32,2,256]{3,1,2,0:T(8,128)(2,1)} %copy.52), calls=%async_computation.1 | async-start | bytes 524288 | tf_op jit(solution)/shard_map/all_to_all | solution.py:84
  86.3 0.7 and_convert_fusion.1
  86.9 0.2 fusion.10
  87.1 0.6 copy-done.7
  87.7 0.8 fusion.25
  88.5 1.1 fusion.41
  89.7 5.9 %custom-call.24 = f32[2,32,32]{2,1,0:T(8,128)S(1)} custom-call(f32[2,32,32]{2,1,0:T(8,128)S(1)} %fusion.24), custom_call_target="Cholesky" | custom-call | tf_op jit(solution)/shard_map/jit(cholesky)/cholesky | solution.py:33
  95.6 0.1 compare_reduce_fusion.2
  95.7 0.1 select_bitcast_fusion.2
  95.8 4.9 %custom-call.25 = f32[2,1,32,32]{2,3,1,0:T(8,128)S(1)} custom-call(f32[2,1,32,32]{3,2,1,0:T(8,128)S(1)} %select_bitcast_fusion.2), custom_call_target="InvertDiagBlocksLowerTriangular" | custom-call | tf_op jit(solution)/shard_map/jit(_solve_triangular)/vmap()/triangular_solve | solution.py:34
  100.7 1.1 convolution_convert_fusion.2
  101.8 2.7 %fusion.8 = f32[2,32,4096]{2,1,0:T(8,128)S(1)} fusion(bf16[2,32,4096]{2,1,0:T(8,128)(2,1)S(1)} %convolution_convert_fusion.2, bf16[1,4096,128]{2,1,0:T(8,128)(2,1)} %bitcast.166, bf16[1,4096,128]{2,1,0:T(8,128)(2,1)S(1)} %bitcast.162), kind=kOutput, calls=%fused_computation.29 | convolution fusion | flops 136323072 | bytes 3670016 | tf_op jit(solution)/shard_map/prf,pkf->prk/dot_general | solution.py:24
  104.5 1.1 fusion.42
  105.7 5.9 %custom-call.26 = f32[2,32,32]{2,1,0:T(8,128)S(1)} custom-call(f32[2,32,32]{2,1,0:T(8,128)S(1)} %fusion.22), custom_call_target="Cholesky" | custom-call | tf_op jit(solution)/shard_map/jit(cholesky)/cholesky | solution.py:33
  111.6 0.1 compare_reduce_fusion.1
  111.7 0.1 select_bitcast_fusion.1
  111.8 4.9 %custom-call.27 = f32[2,1,32,32]{2,3,1,0:T(8,128)S(1)} custom-call(f32[2,1,32,32]{3,2,1,0:T(8,128)S(1)} %select_bitcast_fusion.1), custom_call_target="InvertDiagBlocksLowerTriangular" | custom-call | tf_op jit(solution)/shard_map/jit(_solve_triangular)/vmap()/triangular_solve | solution.py:34
  116.7 1.1 convolution_convert_fusion.1
  117.8 2.7 %fusion.9 = f32[2,32,4096]{2,1,0:T(8,128)S(1)} fusion(bf16[2,32,4096]{2,1,0:T(8,128)(2,1)S(1)} %convolution_convert_fusion.1, bf16[1,4096,128]{2,1,0:T(8,128)(2,1)} %bitcast.167, bf16[1,4096,128]{2,1,0:T(8,128)(2,1)S(1)} %bitcast.163), kind=kOutput, calls=%fused_computation.30 | convolution fusion | flops 136323072 | bytes 3670016 | tf_op jit(solution)/shard_map/prf,pkf->prk/dot_general | solution.py:24
  120.5 1.1 fusion.43
  121.7 5.9 %custom-call.28 = f32[2,32,32]{2,1,0:T(8,128)S(1)} custom-call(f32[2,32,32]{2,1,0:T(8,128)S(1)} %fusion.20), custom_call_target="Cholesky" | custom-call | tf_op jit(solution)/shard_map/jit(cholesky)/cholesky | solution.py:33
  127.6 0.1 compare_reduce_fusion
  127.7 0.1 select_bitcast_fusion
  127.8 5.1 %custom-call.29 = f32[2,1,32,32]{2,3,1,0:T(8,128)S(1)} custom-call(f32[2,1,32,32]{3,2,1,0:T(8,128)S(1)} %select_bitcast_fusion), custom_call_target="InvertDiagBlocksLowerTriangular" | custom-call | tf_op jit(solution)/shard_map/jit(_solve_triangular)/vmap()/triangular_solve | solution.py:34
  132.9 1.0 convolution_convert_fusion
  133.9 0.1 copy.75
  134.1 1.7 fusion
  135.8 0.1 copy.71
  136.0 1.8 %fusion.1 = bf16[8,32,2,32]{1,0,3,2:T(8,128)(2,1)S(1)} fusion(f32[8,32,2,8]{1,3,0,2:T(8,128)S(1)} %copy-done.4, bf16[2,32,16,256]{3,2,1,0:T(8,128)(2,1)S(1)} %bitcast.171, bf16[8,32,2,256]{3,1,2,0:T(8,128)(2,1)} %all-to-all-done.1), kind=kOutput, calls=%fused_computation.17 | convolution fusion | flops 67354624 | bytes 491520 | tf_op jit(solution)/shard_map/nkb,prgb->nkpgr/dot_general | solution.py:90
  137.8 0.1 copy.70
  138.0 0.8 reshape.619
  138.8 5.1 %all-to-all-start.2 = ((bf16[8,2,2048]{2,1,0:T(2,128)(2,1)}), bf16[8,2,2048]{2,1,0:T(2,128)(2,1)S(1)}, u32[]{:S(2)}, u32[]{:S(2)}) async-start(bf16[8,2,2048]{2,1,0:T(2,128)(2,1)} %reshape.619), calls=%async_computation.2 | async-start | bytes 131072 | tf_op jit(solution)/shard_map/all_to_all | solution.py:110
  143.9 1.1 fusion.40
  145.0 14.5 %all_gather.11 = bf16[16,32,128]{2,1,0:T(8,128)(2,1)S(1)} all-gather(bf16[2,32,128]{2,1,0:T(8,128)(2,1)S(1)} %get-tuple-element.26), channel_id=1, replica_groups=mesh['plane'=4,'tile'=8] {'tile'}, dimensions={0}, use_global_device_ids=true | all-gather | bytes 147456 | tf_op jit(solution)/shard_map/all_gather | solution.py:117
  159.5 0.1 reshape.620
  159.6 0.1 copy.58
  159.7 1.0 gather_fusion.1
  160.7 0.1 copy.60
  160.8 1.0 gather_fusion
  161.9 0.1 copy.59
  162.1 0.2 copy.61
  162.2 10.6 %gather_fusion.2 = bf16[2048,32]{1,0:T(8,128)(2,1)S(1)} fusion(bf16[128,5,32]{2,0,1:T(8,128)(2,1)S(1)} %copy.61, s32[2048]{0:T(1024)S(1)} %reshape.579), kind=kCustom, calls=%fused_computation.2 | custom fusion | bytes 278528 | tf_op jit(solution)/shard_map/jit(take_along_axis)/gather | solution.py:131
  172.8 0.4 copy.62
  173.3 0.9 fusion.7
  (55 shorter events, 0.8 us)
Async XLA Ops:
  0.6 44.8 %copy-start = (bf16[1,1,3,4,256,128]{5,4,3,2,1,0:T(8,128)(2,1)S(1)}, bf16[1,1,3,4,256,128]{5,4,3,2,1,0:T(8,128)(2,1)}, u32[]{:S(2)}) copy-start(bf16[1,1,3,4,256,128]{5,4,3,2,1,0:T(8,128)(2,1)} %param.8) | copy-start | bytes 2359300
  0.6 46.3 %copy-start.5 = (s32[1,128,1]{1,2,0:T(1,128)S(1)}, s32[1,128,1]{1,2,0:T(1,128)}, u32[]{:S(2)}) copy-start(s32[1,128,1]{1,2,0:T(1,128)} %param.11) | copy-start | bytes 1540
  2.3 45.1 %copy-start.6 = (s32[1,128]{1,0:T(1,128)S(1)}, s32[1,128]{1,0:T(1,128)}, u32[]{:S(2)}) copy-start(s32[1,128]{1,0:T(1,128)} %param.12) | copy-start | bytes 1540
  45.6 41.3 %collective-permute-start = (bf16[3,4,256,128]{3,2,1,0:T(8,128)(2,1)S(1)}, bf16[3,4,256,128]{3,2,1,0:T(8,128)(2,1)S(1)}, u32[]{:S(2)}, u32[]{:S(2)}) collective-permute-start(bf16[3,4,256,128]{3,2,1,0:T(8,128)(2,1)S(1)} %fusion.5), channel_id=1, source_target_pairs={{2,0},{3,1},{4,2},{5,3},{6,4},{7,5},{10,8},{11,9},{12,10},{13,11},... | collective-permute-start | bytes 2359304 | tf_op jit(solution)/shard_map/ppermute | solution.py:17
  61.1 5.2 %copy-start.3 = (bf16[1,128,256]{2,1,0:T(8,128)(2,1)S(1)}, bf16[1,128,256]{2,1,0:T(8,128)(2,1)}, u32[]{:S(2)}) copy-start(bf16[1,128,256]{2,1,0:T(8,128)(2,1)} %param.10) | copy-start | bytes 196612
  61.8 19.1 %all-to-all-start = ((s32[8,32,2]{1,2,0:T(2,128)}), s32[8,32,2]{1,2,0:T(2,128)S(1)}, u32[]{:S(2)}, u32[]{:S(2)}) async-start(s32[8,32,2]{1,2,0:T(2,128)} %copy.50), calls=%async_computation | async-start | bytes 16384 | tf_op jit(solution)/shard_map/all_to_all | solution.py:85
  80.9 53.1 %all-to-all-start.1 = ((bf16[8,32,2,256]{3,1,2,0:T(8,128)(2,1)}), bf16[8,32,2,256]{3,1,2,0:T(8,128)(2,1)}, u32[]{:S(2)}, u32[]{:S(2)}) async-start(bf16[8,32,2,256]{3,1,2,0:T(8,128)(2,1)} %copy.52), calls=%async_computation.1 | async-start | bytes 524288 | tf_op jit(solution)/shard_map/all_to_all | solution.py:84
  86.9 0.8 copy-start.7
  87.1 1.4 copy-start.1
  134.0 1.9 %copy-start.4 = (f32[8,32,2,8]{1,3,0,2:T(8,128)S(1)}, f32[8,32,2,8]{1,3,0,2:T(8,128)}, u32[]{:S(2)}) copy-start(f32[8,32,2,8]{1,3,0,2:T(8,128)} %and_convert_fusion.1) | copy-start | bytes 49156
  136.0 7.9 %copy-start.2 = (bf16[2,2,4,256,128]{4,3,2,1,0:T(8,128)(2,1)S(1)}, bf16[2,2,4,256,128]{4,3,2,1,0:T(8,128)(2,1)}, u32[]{:S(2)}) copy-start(bf16[2,2,4,256,128]{4,3,2,1,0:T(8,128)(2,1)} %copy-done.1) | copy-start | bytes 3145732
  138.8 20.7 %all-to-all-start.2 = ((bf16[8,2,2048]{2,1,0:T(2,128)(2,1)}), bf16[8,2,2048]{2,1,0:T(2,128)(2,1)S(1)}, u32[]{:S(2)}, u32[]{:S(2)}) async-start(bf16[8,2,2048]{2,1,0:T(2,128)(2,1)} %reshape.619), calls=%async_computation.2 | async-start | bytes 131072 | tf_op jit(solution)/shard_map/all_to_all | solution.py:110
